TPU v7x, 32 devices: a whole 2x2x4 slice. The times are simulated.
32 devices in a mesh: fsdp: 8 (over z, x), ctx: 4 (over y, core).
Axes of the slice: x: 2, y: 2, z: 4, core: 2. Of those that a mesh axis runs over, the one named last changes fastest.
Arguments:
- inputs: bfloat16 [8, 1024, 2048], P('fsdp', 'ctx'), may hold values from -6 to 6
- cotangent: bfloat16 [8, 1024, 2048], P('fsdp', 'ctx'), may hold values from -6 to 6
- lengths: int32 [8], P('fsdp'), may hold values from 1024 to 1024, as said below
- qkv_weight: bfloat16 [2048, 1536], P('fsdp'), may hold values from -0.125 to 0.125
- out_weight: bfloat16 [1024, 2048], P('fsdp'), may hold values from -3 to 3
- gate_up: bfloat16 [2048, 2, 4096], P('fsdp'), may hold values from -0.125 to 0.125
- down_weight: bfloat16 [4096, 2048], P('fsdp'), may hold values from -0.09375 to 0.09375
- attn_gain: bfloat16 [2048], P('fsdp'), may hold values from 0.5 to 1.5
- ffn_gain: bfloat16 [2048], P('fsdp'), may hold values from 0.5 to 1.5
- qk_gain: bfloat16 [2, 64], replicated, may hold values from 0.5 to 1.5
Outputs:
- layer_out: bfloat16 [8, 1024, 2048], P('fsdp', 'ctx')
- input_grad: bfloat16 [8, 1024, 2048], P('fsdp', 'ctx')
- qkv_grad: float32 [2048, 1536], P('fsdp')
- out_grad: float32 [1024, 2048], P('fsdp')
- gate_up_grad: float32 [2048, 2, 4096], P('fsdp')
- down_grad: float32 [4096, 2048], P('fsdp')
- attn_gain_grad: float32 [2048], P('fsdp')
- ffn_gain_grad: float32 [2048], P('fsdp')
- qk_gain_grad: float32 [2, 64], replicated
Inputs may be any that keep to these rules, and one draw needn't show every extreme that they name: `lengths`: valid length of each slot; some slot is full, of length 1024.
All inputs are finite; a program needn't handle non-finite values.
Results may differ from a plain program's by a relative error of at most 0.02.
Values may be sent and summed in bfloat16 or wider, within the bound.
A program may use at most 384 MiB of HBM per device.

v0:
```python
import math
import jax
import jax.numpy as jnp
from jax import lax
from jax.sharding import PartitionSpec as P

HEADS = 16
KV_HEADS = 4
HEAD_DIM = 64
EPSILON = 1e-06


def root_norm(values, norm_gain):
    factor = lax.rsqrt(jnp.mean(values * values, axis=-1, keepdims=True) + EPSILON)
    return values * factor * norm_gain


def rotation_tables(positions):
    half_dim = HEAD_DIM // 2
    frequency = 10000.0 ** (-(2.0 * jnp.arange(half_dim, dtype=jnp.float32)) / HEAD_DIM)
    angles = positions.astype(jnp.float32)[:, None] * frequency[None, :]
    return (jnp.cos(angles), jnp.sin(angles))


def rotate(values, cos_table, sin_table):
    half_dim = values.shape[-1] // 2
    lower_half = values[..., :half_dim]
    upper_half = values[..., half_dim:]
    cos_part = cos_table[:, None, :]
    sin_part = sin_table[:, None, :]
    return jnp.concatenate(
        [
            lower_half * cos_part - upper_half * sin_part,
            upper_half * cos_part + lower_half * sin_part,
        ],
        axis=-1,
    )


def prepare_heads(qkv_out, head_gain, cos_table, sin_table):
    row_count = qkv_out.shape[0]
    query_cols = HEADS * HEAD_DIM
    key_cols = KV_HEADS * HEAD_DIM
    queries = qkv_out[:, :query_cols].reshape(row_count, HEADS, HEAD_DIM)
    key_part = qkv_out[:, query_cols : query_cols + key_cols].reshape(row_count, KV_HEADS, HEAD_DIM)
    value_part = qkv_out[:, query_cols + key_cols :]
    queries = rotate(root_norm(queries, head_gain[0]), cos_table, sin_table).reshape(
        row_count, query_cols
    )
    key_part = rotate(root_norm(key_part, head_gain[1]), cos_table, sin_table).reshape(
        row_count, key_cols
    )
    return (queries, key_part, value_part)


def activate(projected):
    gate_part = projected[:, 0]
    return gate_part * jax.nn.sigmoid(gate_part) * projected[:, 1]


def contract_rows(left, right):
    return lax.dot_general(
        left, right, (((0,), (0,)), ((), ())), preferred_element_type=jnp.float32
    )


def contract_cols(left, right):
    return lax.dot_general(
        left, right, (((1,), (1,)), ((), ())), preferred_element_type=jnp.float32
    )


def on_device(
    inputs,
    cotangent,
    lengths,
    qkv_weight,
    out_weight,
    gate_up,
    down_weight,
    attn_gain,
    ffn_gain,
    qk_gain,
):
    token_count = inputs.shape[1]
    group = HEADS // KV_HEADS
    key_cols = KV_HEADS * HEAD_DIM
    seq_len = token_count * lax.axis_size("ctx")
    positions = lax.axis_index("ctx") * token_count + jnp.arange(token_count, dtype=jnp.int32)
    length = lengths[0]
    row_keep = (positions < length).astype(jnp.float32)[:, None]
    inv_root = 1.0 / math.sqrt(HEAD_DIM)
    source = inputs[0].astype(jnp.float32)
    qkv_full, out_full, attn_full, ffn_full = (
        lax.all_gather(qkv_weight, "fsdp", axis=0, tiled=True),
        lax.all_gather(out_weight, "fsdp", axis=0, tiled=True),
        lax.all_gather(attn_gain, "fsdp", axis=0, tiled=True),
        lax.all_gather(ffn_gain, "fsdp", axis=0, tiled=True),
    )
    attn_norm = attn_full.astype(jnp.float32)
    ffn_norm = ffn_full.astype(jnp.float32)
    normed = root_norm(source, attn_norm).astype(jnp.bfloat16)
    qkv_out = jnp.dot(normed, qkv_full, preferred_element_type=jnp.float32)
    cos_table, sin_table = rotation_tables(positions)
    head_gain = qk_gain.astype(jnp.float32)

    def head_pieces(qkv_values, gain_values):
        return prepare_heads(qkv_values, gain_values, cos_table, sin_table)

    head_values, head_pull = jax.vjp(head_pieces, qkv_out, head_gain)
    queries, key_part, value_part = head_values
    query_low = queries.astype(jnp.bfloat16).reshape(token_count, KV_HEADS, group, HEAD_DIM)
    kv_local = jnp.concatenate([key_part, value_part], axis=1).astype(jnp.bfloat16)
    kv_whole = lax.all_gather(kv_local, "ctx", axis=0, tiled=True)
    block = 512
    block_total = seq_len // block
    kv_blocks = kv_whole.reshape(block_total, block, 2, KV_HEADS, HEAD_DIM)
    starts = jnp.arange(block_total, dtype=jnp.int32) * block

    def block_scores(key_block, block_start):
        scores = (
            jnp.einsum("bhgd,thd->hgbt", query_low, key_block, preferred_element_type=jnp.float32)
            * inv_root
        )
        key_pos = block_start + jnp.arange(key_block.shape[0], dtype=jnp.int32)
        visible = (key_pos[None, :] <= positions[:, None]) & (key_pos[None, :] < length)
        return (scores, visible)

    def max_step(state, item):
        running_max, running_sum = state
        kv_block, block_start = item
        scores, visible = block_scores(kv_block[:, 0], block_start)
        new_max = jnp.maximum(running_max, jnp.max(jnp.where(visible, scores, -1e30), axis=-1))
        expanded = jnp.where(visible, jnp.exp(scores - new_max[..., None]), 0.0)
        running_sum = running_sum * jnp.exp(running_max - new_max) + jnp.sum(expanded, axis=-1)
        return ((new_max, running_sum), None)

    stat_shape = (KV_HEADS, group, token_count)
    start_state = (jnp.full(stat_shape, -1e30, jnp.float32), jnp.zeros(stat_shape, jnp.float32))
    final_state, unused_out = lax.scan(max_step, start_state, (kv_blocks, starts))
    log_total = final_state[0] + jnp.log(final_state[1])

    def block_probs(kv_block, block_start):
        scores, visible = block_scores(kv_block[:, 0], block_start)
        return jnp.where(visible, jnp.exp(scores - log_total[..., None]), 0.0)

    def value_step(totals, item):
        kv_block, block_start = item
        probs_low = block_probs(kv_block, block_start).astype(jnp.bfloat16)
        return (
            totals
            + jnp.einsum(
                "hgbt,thd->bhgd", probs_low, kv_block[:, 1], preferred_element_type=jnp.float32
            ),
            None,
        )

    attended, unused_out = lax.scan(
        value_step,
        jnp.zeros((token_count, KV_HEADS, group, HEAD_DIM), jnp.float32),
        (kv_blocks, starts),
    )
    attended_low = attended.reshape(token_count, HEADS * HEAD_DIM).astype(jnp.bfloat16)
    middle = source + jnp.dot(attended_low, out_full, preferred_element_type=jnp.float32)
    normed_mid = root_norm(middle, ffn_norm).astype(jnp.bfloat16)
    columns = normed_mid
    projected = jnp.einsum(
        "td,dgf->tgf",
        columns,
        lax.all_gather(gate_up, "fsdp", axis=0, tiled=True),
        preferred_element_type=jnp.float32,
    )
    act_value, act_pull = jax.vjp(activate, projected)
    hidden = act_value.astype(jnp.bfloat16)
    columns = hidden
    ffn_out = jnp.dot(
        columns,
        lax.all_gather(down_weight, "fsdp", axis=0, tiled=True),
        preferred_element_type=jnp.float32,
    )
    layer_out = (row_keep * (middle + ffn_out)).astype(jnp.bfloat16)[None]
    d_out = row_keep * cotangent[0].astype(jnp.float32)
    d_out_low = d_out.astype(jnp.bfloat16)
    down_shard = lax.psum_scatter(
        contract_rows(hidden, d_out_low).astype(jnp.bfloat16),
        "fsdp",
        scatter_dimension=0,
        tiled=True,
    )
    d_hidden = contract_cols(d_out_low, lax.all_gather(down_weight, "fsdp", axis=0, tiled=True))
    d_proj_low = act_pull(d_hidden)[0].astype(jnp.bfloat16)
    columns = normed_mid
    gate_up_shard = lax.psum_scatter(
        jnp.einsum("td,tgf->dgf", columns, d_proj_low, preferred_element_type=jnp.float32).astype(
            jnp.bfloat16
        ),
        "fsdp",
        scatter_dimension=0,
        tiled=True,
    )
    d_normed_mid = jnp.einsum(
        "tgf,dgf->td",
        d_proj_low,
        lax.all_gather(gate_up, "fsdp", axis=0, tiled=True),
        preferred_element_type=jnp.float32,
    )
    mid_value, mid_pull = jax.vjp(root_norm, middle, ffn_norm)
    d_mid_norm, ffn_gain_part = mid_pull(d_normed_mid)
    d_middle = d_out + d_mid_norm
    d_branch = d_middle.astype(jnp.bfloat16)
    out_term = contract_rows(attended_low, d_branch)
    d_attended = (
        contract_cols(d_branch, out_full)
        .astype(jnp.bfloat16)
        .reshape(token_count, KV_HEADS, group, HEAD_DIM)
    )
    delta = jnp.transpose(jnp.sum(d_attended.astype(jnp.float32) * attended, axis=-1), (1, 2, 0))

    def block_grads(kv_block, block_start):
        probs = block_probs(kv_block, block_start)
        d_probs = jnp.einsum(
            "bhgd,thd->hgbt", d_attended, kv_block[:, 1], preferred_element_type=jnp.float32
        )
        d_scores = (probs * (d_probs - delta[..., None])).astype(jnp.bfloat16)
        return (probs.astype(jnp.bfloat16), d_scores)

    def query_step(totals, item):
        kv_block, block_start = item
        probs_low, d_scores = block_grads(kv_block, block_start)
        return (
            totals
            + jnp.einsum(
                "hgbt,thd->bhgd", d_scores, kv_block[:, 0], preferred_element_type=jnp.float32
            ),
            None,
        )

    d_query_sum, unused_out = lax.scan(
        query_step,
        jnp.zeros((token_count, KV_HEADS, group, HEAD_DIM), jnp.float32),
        (kv_blocks, starts),
    )
    d_query = (d_query_sum * inv_root).reshape(token_count, HEADS * HEAD_DIM).astype(jnp.bfloat16)
    sub_block = 512
    sub_total = token_count * lax.axis_size("ctx") // sub_block
    pieces = kv_whole.reshape(sub_total, sub_block, 2, KV_HEADS, HEAD_DIM)
    sub_starts = jnp.arange(sub_total, dtype=jnp.int32) * sub_block

    def key_grads(item):
        kv_block, block_start = item
        probs_low, d_scores = block_grads(kv_block, block_start)
        d_keys = (
            jnp.einsum("hgbt,bhgd->thd", d_scores, query_low, preferred_element_type=jnp.float32)
            * inv_root
        )
        d_values = jnp.einsum(
            "hgbt,bhgd->thd", probs_low, d_attended, preferred_element_type=jnp.float32
        )
        return jnp.concatenate(
            [d_keys.reshape(sub_block, key_cols), d_values.reshape(sub_block, key_cols)], axis=1
        )

    kv_grad = lax.psum_scatter(
        lax.map(key_grads, (pieces, sub_starts))
        .reshape(token_count * lax.axis_size("ctx"), 2 * key_cols)
        .astype(jnp.bfloat16),
        "ctx",
        scatter_dimension=0,
        tiled=True,
    ).astype(jnp.float32)
    d_key_low = kv_grad[:, :key_cols].astype(jnp.bfloat16).astype(jnp.float32)
    d_value_low = kv_grad[:, key_cols:].astype(jnp.bfloat16).astype(jnp.float32)
    d_qkv_out, qk_part = head_pull((d_query.astype(jnp.float32), d_key_low, d_value_low))
    d_qkv = d_qkv_out.astype(jnp.bfloat16)
    qkv_term = contract_rows(normed, d_qkv)
    d_normed = contract_cols(d_qkv, qkv_full)
    first_value, first_pull = jax.vjp(root_norm, source, attn_norm)
    d_source_norm, attn_gain_part = first_pull(d_normed)
    input_grad = (d_middle + d_source_norm).astype(jnp.bfloat16)[None]
    qkv_shard, out_shard, attn_shard, ffn_shard = (
        lax.psum_scatter(
            qkv_term.astype(jnp.bfloat16), "fsdp", scatter_dimension=0, tiled=True
        ).astype(jnp.float32),
        lax.psum_scatter(
            out_term.astype(jnp.bfloat16), "fsdp", scatter_dimension=0, tiled=True
        ).astype(jnp.float32),
        lax.psum_scatter(
            attn_gain_part.astype(jnp.bfloat16), "fsdp", scatter_dimension=0, tiled=True
        ).astype(jnp.float32),
        lax.psum_scatter(
            ffn_gain_part.astype(jnp.bfloat16), "fsdp", scatter_dimension=0, tiled=True
        ).astype(jnp.float32),
    )
    summed = (
        lax.psum(qkv_shard.astype(jnp.bfloat16), "ctx").astype(jnp.float32),
        lax.psum(out_shard.astype(jnp.bfloat16), "ctx").astype(jnp.float32),
        lax.psum(gate_up_shard, "ctx").astype(jnp.float32),
        lax.psum(down_shard, "ctx").astype(jnp.float32),
        lax.psum(attn_shard.astype(jnp.bfloat16), "ctx").astype(jnp.float32),
        lax.psum(ffn_shard.astype(jnp.bfloat16), "ctx").astype(jnp.float32),
    )
    qk_total = lax.psum(qk_part, ("fsdp", "ctx"))
    return (
        layer_out,
        input_grad,
        summed[0],
        summed[1],
        summed[2],
        summed[3],
        summed[4],
        summed[5],
        qk_total,
    )


def solution(mesh):
    return jax.shard_map(
        on_device,
        mesh=mesh,
        in_specs=(
            P("fsdp", "ctx", None),
            P("fsdp", "ctx", None),
            P("fsdp"),
            P("fsdp", None),
            P("fsdp", None),
            P("fsdp", None, None),
            P("fsdp", None),
            P("fsdp"),
            P("fsdp"),
            P(),
        ),
        out_specs=(
            P("fsdp", "ctx", None),
            P("fsdp", "ctx", None),
            P("fsdp", None),
            P("fsdp", None),
            P("fsdp", None, None),
            P("fsdp", None),
            P("fsdp"),
            P("fsdp"),
            P(),
        ),
        check_vma=False,
    )
```

profile of v0, /device:TPU:0, one launch (start us, length us, event | category | flops | bytes accessed | tf_op | source)
XLA Modules:
  0.0 2385.9 jit_solution(13541562072520986390)
XLA Ops:
  8.6 22.5 all-gather
  34.1 77.8 %all-gather.8.cloned.1.call-done = bf16[2048,1536]{1,0:T(8,128)(2,1)} async-done(((bf16[256,1536]{1,0:T(8,128)(2,1)}), bf16[2048,1536]{1,0:T(8,128)(2,1)}) %all-gather.8.cloned.1.call-update) | async-done | bytes 6291472 | tf_op jit(solution)/shard_map/all_gather | solution.py:95
  128.4 17.9 all-gather.1
  157.6 25.6 %while.47 = (s32[]{:T(128)}, f32[4,4,256]{2,1,0:T(4,128)S(1)}, f32[4,4,256]{2,1,0:T(4,128)S(1)}, s32[2]{0:T(128)S(1)}, s32[]{:T(128)}, /*index=5*/bf16[2,512,2,4...) while((s32[]{:T(128)}, f32[4,4,256]{2,1,0:T(4,128)S(1)}, ...), condition=%wide.region_6.7_spmd.clone, body=%wide.region_3.6_spmd.clone.sunk | while | flops 283399936 | bytes 19225752 | solution.py:140
  183.2 13.6 while.48
  198.1 12.3 all-gather.12.cloned.1.call-done
  215.3 633.1 %all-gather.14.cloned.1.call-done = bf16[2048,2,4096]{2,0,1:T(8,128)(2,1)} async-done(((bf16[256,2,4096]{2,0,1:T(8,128)(2,1)}), bf16[2048,2,4096]{2,0,1:T(8,128)(2,1)}) %all-gather.14.cloned.1.call-update) | async-done | bytes 33554448 | tf_op jit(solution)/shard_map/all_gather | solution.py:170
  848.4 20.3 fusion.110
  868.8 209.3 %all-gather.16.cloned.1.call-done = bf16[4096,2048]{1,0:T(8,128)(2,1)} async-done(((bf16[512,2048]{1,0:T(8,128)(2,1)}), bf16[4096,2048]{1,0:T(8,128)(2,1)}) %all-gather.16.cloned.1.call-update) | async-done | bytes 16777232 | tf_op jit(solution)/shard_map/all_gather | solution.py:178
  1078.0 13.2 multiply_bitcast_fusion
  1091.3 18.9 multiply_reduce_fusion
  1119.4 29.0 %while.46 = (s32[]{:T(128)}, bf16[2,512,512]{2,1,0:T(8,128)(2,1)}, s32[2]{0:T(128)S(1)}, s32[]{:T(128)}, bf16[2,512,2,4,64]{1,4,3,2,0:T(8,128)(2,1)S(1)}, /*inde...) while((s32[]{:T(128)}, bf16[2,512,512]{2,1,0:T(8,128)(2,1)}, ...), condition=%wide.region_13.14_spmd.clone, body=%wide.region_12.13_spmd.clone.sunk | while | flops 1096288000 | bytes 68607184 | solution.py:264
  1154.5 30.2 %while.49 = (s32[]{:T(128)}, f32[256,4,4,64]{0,3,2,1:T(8,128)}, bf16[2,512,2,4,64]{1,4,3,2,0:T(8,128)(2,1)S(1)}, s32[2]{0:T(128)S(1)}, s32[]{:T(128)}, /*index=5...) while((s32[]{:T(128)}, f32[256,4,4,64]{0,3,2,1:T(8,128)}, ...), condition=%wide.region_17.18_spmd.clone, body=%wide.region_16.17_spmd.clone.sunk | while | flops 818677504 | bytes 22060200 | solution.py:238
  1198.7 12.5 convolution_convert_fusion.1
  1212.8 17.8 convolution_convert_fusion
  1230.7 33.2 %reduce-scatter.10.cloned.1.call-done = bf16[128,2048]{1,0:T(8,128)(2,1)} async-done(((bf16[1024,2048]{1,0:T(8,128)(2,1)}), bf16[128,2048]{1,0:T(8,128)(2,1)}) %reduce-scatter.10.cloned.1.call-update) | async-done | bytes 524304 | tf_op jit(solution)/shard_map/reduce_scatter | solution.py:284
  1263.9 121.3 %reduce-scatter.8.cloned.1.call-done = bf16[256,1536]{1,0:T(8,128)(2,1)} async-done(((bf16[2048,1536]{1,0:T(8,128)(2,1)}), bf16[256,1536]{1,0:T(8,128)(2,1)}) %reduce-scatter.8.cloned.1.call-update) | async-done | bytes 786448 | tf_op jit(solution)/shard_map/reduce_scatter | solution.py:281
  1385.2 285.7 %reduce-scatter.14.cloned.1.call-done = bf16[512,2048]{1,0:T(8,128)(2,1)} async-done(((bf16[4096,2048]{1,0:T(8,128)(2,1)}), bf16[512,2048]{1,0:T(8,128)(2,1)}) %reduce-scatter.14.cloned.1.call-update) | async-done | bytes 2097168 | tf_op jit(solution)/shard_map/reduce_scatter | solution.py:184
  1671.0 546.2 %reduce-scatter.12.cloned.1.call-done = bf16[256,2,4096]{2,0,1:T(8,128)(2,1)} async-done(((bf16[2048,2,4096]{2,0,1:T(8,128)(2,1)}), bf16[256,2,4096]{2,0,1:T(8,128)(2,1)}) %reduce-scatter.12.cloned.1.call-update) | async-done | bytes 4194320 | tf_op jit(solution)/shard_map/reduce_scatter | solution.py:193
  2218.4 15.3 fusion.83
  2240.6 19.1 all-reduce.13
  2268.2 38.0 %psum.55 = f32[2,64]{1,0:T(2,128)} all-reduce(f32[2,64]{1,0:T(2,128)S(1)} %pad_add_fusion.2), channel_id=1, replica_groups=mesh['fsdp'=8,'ctx'=4] {'fsdp','ctx'}, use_global_device_ids=true, to_apply=%region_36.37 | all-reduce | flops 128 | bytes 1024 | tf_op jit(solution)/shard_map/psum | solution.py:302
  2310.1 51.8 %all-reduce.18.cloned.1.call-done = (bf16[256,2,4096]{2,0,1:T(8,128)(2,1)}, bf16[256,1536]{1,0:T(8,128)(2,1)}, bf16[128,2048]{1,0:T(8,128)(2,1)}, bf16[512,2048]{1,0:T(8,128)(2,1)}) async-done(((bf16[256,2,4096]{2,0,1:T(8,128)(2,1)}, bf16[256,1536]{1,0:T(8,128)(2,1)}, bf16[128,2048]{1,0:T(8,128)(2,1)}, bf16[512,2048]{1,0:T(8,128)(2,1)}), (bf16[256,2,4096]{2,0,1:T(8,128)(2,1)}, bf16[256,1536]{1,0:T(8,128)(2,1)}, ...) | async-done | bytes 7602192 | tf_op jit(solution)/shard_map/psum | solution.py:297
  2366.5 10.1 copy.74
  (281 shorter events, 192.2 us)
Async XLA Ops:
  7.2 104.8 %all-gather.8.cloned.1.call-start = ((), (), s32[]{:S(2)}) async-start(), calls=%async_computation.5 | async-start | bytes 7077888 | tf_op jit(solution)/shard_map/all_gather | solution.py:95
  7.9 142.1 %all-gather.10.cloned.1.call-start = ((), (), s32[]{:S(2)}) async-start(), calls=%async_computation.6 | async-start | bytes 1310720 | tf_op jit(solution)/shard_map/all_gather | solution.py:114
  31.1 85.8 %copy-start.27 = (f32[8,1,256]{2,1,0:T(1,128)}, f32[8,1,256]{2,1,0:T(1,128)S(1)}, u32[]{:S(2)}) copy-start(f32[8,1,256]{2,1,0:T(1,128)S(1)} %convert_element_type.220) | copy-start | bytes 24580
  33.9 83.1 %copy-start.36 = (f32[256]{0:T(256)}, f32[256]{0:T(256)S(1)}, u32[]{:S(2)}) copy-start(f32[256]{0:T(256)S(1)} %fusion.115) | copy-start | bytes 3076
  33.9 84.4 %copy-start.41 = (f32[64]{0:T(128)}, f32[64]{0:T(128)S(1)}, u32[]{:S(2)}) copy-start(f32[64]{0:T(128)S(1)} %get-tuple-element.562) | copy-start | bytes 772
  33.9 114.9 %copy-start.43 = (f32[64]{0:T(128)}, f32[64]{0:T(128)S(1)}, u32[]{:S(2)}) copy-start(f32[64]{0:T(128)S(1)} %get-tuple-element.561) | copy-start | bytes 772
  34.1 115.7 %copy-start.21 = (f32[256,32]{0,1:T(8,128)}, f32[256,32]{0,1:T(8,128)S(1)}, u32[]{:S(2)}) copy-start(f32[256,32]{0,1:T(8,128)S(1)} %get-tuple-element.559) | copy-start | bytes 98308
  34.1 115.7 %copy-start.23 = (f32[256,32]{0,1:T(8,128)}, f32[256,32]{0,1:T(8,128)S(1)}, u32[]{:S(2)}) copy-start(f32[256,32]{0,1:T(8,128)S(1)} %get-tuple-element.560) | copy-start | bytes 98308
  119.8 90.6 %all-gather.12.cloned.1.call-start = ((), (), s32[]{:S(2)}) async-start(), calls=%async_computation.7 | async-start | bytes 4718592 | tf_op jit(solution)/shard_map/all_gather | solution.py:96
  120.6 727.9 %all-gather.14.cloned.1.call-start = ((), (), s32[]{:S(2)}) async-start(), calls=%async_computation.8 | async-start | bytes 37748736 | tf_op jit(solution)/shard_map/all_gather | solution.py:170
  127.7 950.3 %all-gather.16.cloned.1.call-start = ((), (), s32[]{:S(2)}) async-start(), calls=%async_computation.9 | async-start | bytes 18874368 | tf_op jit(solution)/shard_map/all_gather | solution.py:178
  128.3 1062.0 %reduce-scatter.6.cloned.1.call-start = ((), (), s32[]{:S(2)}) async-start(), calls=%async_computation.10 | async-start | bytes 1310720 | tf_op jit(solution)/shard_map/reduce_scatter | solution.py:263
  147.0 963.2 %copy-start.45 = (f32[256]{0:T(256)}, f32[256]{0:T(256)S(1)}, u32[]{:S(2)}) copy-start(f32[256]{0:T(256)S(1)} %compare_convert_fusion) | copy-start | bytes 3076
  215.3 894.9 %copy-start.31 = (f32[256]{0:T(256)}, f32[256]{0:T(256)S(1)}, u32[]{:S(2)}) copy-start(f32[256]{0:T(256)S(1)} %fusion.116) | copy-start | bytes 3076
  848.4 229.6 %copy-start.19 = (bf16[1,256,2048]{2,1,0:T(8,128)(2,1)S(1)}, bf16[1,256,2048]{2,1,0:T(8,128)(2,1)}, u32[]{:S(2)}) copy-start(bf16[1,256,2048]{2,1,0:T(8,128)(2,1)} %param.19) | copy-start | bytes 3145732
  1148.5 115.4 %reduce-scatter.10.cloned.1.call-start = ((), (), s32[]{:S(2)}) async-start(), calls=%async_computation.12 | async-start | bytes 4718592 | tf_op jit(solution)/shard_map/reduce_scatter | solution.py:284
  1153.4 231.8 %reduce-scatter.8.cloned.1.call-start = ((), (), s32[]{:S(2)}) async-start(), calls=%async_computation.11 | async-start | bytes 7077888 | tf_op jit(solution)/shard_map/reduce_scatter | solution.py:281
  1197.4 473.5 %reduce-scatter.14.cloned.1.call-start = ((), (), s32[]{:S(2)}) async-start(), calls=%async_computation.14 | async-start | bytes 18874368 | tf_op jit(solution)/shard_map/reduce_scatter | solution.py:184
  1211.2 1005.9 %reduce-scatter.12.cloned.1.call-start = ((), (), s32[]{:S(2)}) async-start(), calls=%async_computation.13 | async-start | bytes 37748736 | tf_op jit(solution)/shard_map/reduce_scatter | solution.py:193
  1230.7 986.5 %copy-start.49 = (u32[32]{0:T(128)S(1)}, u32[32]{0:T(128)}, u32[]{:S(2)}) copy-start(u32[32]{0:T(128)} %constant.125) | copy-start | bytes 388
  1230.7 987.7 %copy-start.47 = (f32[256]{0:T(256)S(1)}, f32[256]{0:T(256)}, u32[]{:S(2)}) copy-start(f32[256]{0:T(256)} %copy-done.45) | copy-start | bytes 3076
  1230.7 1131.2 %all-reduce.18.cloned.1.call-start = ((), (), s32[]{:S(2)}) async-start(), calls=%async_computation.15 | async-start | bytes 15204352 | tf_op jit(solution)/shard_map/psum | solution.py:297
  2233.8 72.4 %copy-start.40 = (f32[256]{0:T(256)S(1)}, f32[256]{0:T(256)}, u32[]{:S(2)}) copy-start(f32[256]{0:T(256)} %copy-done.39) | copy-start | bytes 3076
  2233.8 73.1 %copy-start.8 = (f32[256,2048]{1,0:T(8,128)S(1)}, f32[256,2048]{1,0:T(8,128)}, u32[]{:S(2)}) copy-start(f32[256,2048]{1,0:T(8,128)} %copy-done.7) | copy-start | bytes 6291460
  (39 other events, 248.2 us)
Sparse Core Ops, SparseCore 0:
  10.2 101.7 all-gather.7
  119.9 14.9 all-gather.9
  137.0 73.3 all-gather.11
  212.4 635.9 all-gather.13
  850.4 227.5 all-gather.15
  1148.6 23.0 reduce-scatter.5
  1175.8 88.0 reduce-scatter.9
  1267.5 117.7 reduce-scatter.7
  1389.0 281.8 reduce-scatter.13
  1675.0 542.0 reduce-scatter.11
  2219.8 142.0 all-reduce.17
where the time goes:
time: 2390 us
  waiting for transfers between devices  1970 us (82%)
  matrix products  189 us (8%)
  blocking collectives  104 us (4%)
  other arithmetic  55.1 us (2%)
  local copies, waits for them, and re-layouts  47.4 us (2%)
    all_gather x1, waiting for transfers between devices, on_device(): lax.all_gather(gate_up, 'fsdp', axis=0, tiled=True)  633 us
    reduce_scatter x1, waiting for transfers between devices, on_device(): lax.psum_scatter(jnp.einsum('td,tgf->dgf', columns, d_proj_low, preferred...  546 us
    reduce_scatter x1, waiting for transfers between devices, on_device(): lax.psum_scatter(contract_rows(hidden, d_out_low).astype(jnp.bfloat16), '...  286 us
    all_gather x1, waiting for transfers between devices, on_device(): lax.all_gather(down_weight, 'fsdp', axis=0, tiled=True)  209 us
    reduce_scatter x1, waiting for transfers between devices, on_device(): lax.psum_scatter(qkv_term.astype(jnp.bfloat16), 'fsdp', scatter_dimension...  121 us
    all_gather x1, waiting for transfers between devices, on_device(): lax.all_gather(qkv_weight, 'fsdp', axis=0, tiled=True)  77.8 us
    psum x1, waiting for transfers between devices, on_device(): lax.psum(gate_up_shard, 'ctx').astype(jnp.float32)  51.8 us
  transfers between devices with their start and end apart: 11, of which 9 were waited for; matrix products, arithmetic and copies ran while one was open for 8% of the time, Pallas kernels for 0%

commit v1 on v0

--- a/solution.py
+++ b/solution.py
@@ -8,6 +8,18 @@
 KV_HEADS = 4
 HEAD_DIM = 64
 EPSILON = 1e-06
+
+
+def gather_by_bits(shard, axis, dim):
+    ways, here, step = (lax.axis_size(axis), lax.axis_index(axis), shard.shape[dim])
+    line, have = (shard, 1)
+    while have < ways:
+        line = jnp.concatenate(
+            [line, lax.ppermute(line, axis, [(d, (d - have) % ways) for d in range(ways)])],
+            axis=dim,
+        )
+        have = 2 * have
+    return jnp.roll(line, here * step, axis=dim)
 
 
 def root_norm(values, norm_gain):
@@ -167,7 +179,7 @@
     projected = jnp.einsum(
         "td,dgf->tgf",
         columns,
-        lax.all_gather(gate_up, "fsdp", axis=0, tiled=True),
+        gather_by_bits(gate_up, "fsdp", 0),
         preferred_element_type=jnp.float32,
     )
     act_value, act_pull = jax.vjp(activate, projected)

time: 2390 us -> 3150 us (1.32)
  blocking collectives: 104 us -> 501 us
  waiting for transfers between devices: 1970 us -> 2240 us
  local copies, waits for them, and re-layouts: 47.4 us -> 104 us
    ppermute x0 -> x3, waiting for transfers between devices: none -> 1000 us  [gather_by_bits(): lax.ppermute(line, axis, [(d, (d - have) % ways) for d in range(ways)])]
    all_gather x1, waiting for transfers between devices: 633 us -> 71.4 us  [on_device(): lax.all_gather(gate_up, 'fsdp', axis=0, tiled=True)]
    all_gather x1, blocking collectives: 17.9 us -> 415 us  [on_device(): lax.all_gather(ffn_gain, 'fsdp', axis=0, tiled=True)]
    all_gather x1, waiting for transfers between devices: 209 us -> 0.01 us  [on_device(): lax.all_gather(down_weight, 'fsdp', axis=0, tiled=True)]
    reduce_scatter x1, waiting for transfers between devices: 33.2 us -> 91.1 us  [on_device(): lax.psum_scatter(out_term.astype(jnp.bfloat16), 'fsdp', scatter_dimension...]
    unnamed x104 -> x118, local copies, waits for them, and re-layouts: 29.6 us -> 74.5 us
  transfers between devices with their start and end apart: 11 -> 14, of which waited for: 9 -> 11; matrix products, arithmetic and copies ran while one was open for 8% -> 9% of each run, Pallas kernels for 0% -> 0%
where the time goes in v1:
time: 3150 us; the launch traced here: 3140 us
  waiting for transfers between devices  2240 us (71%)
  blocking collectives  501 us (16%)
  matrix products  199 us (6%)
  local copies, waits for them, and re-layouts  104 us (3%)
  other arithmetic  72.4 us (2%)
    ppermute x3, waiting for transfers between devices, gather_by_bits(): lax.ppermute(line, axis, [(d, (d - have) % ways) for d in range(ways)])  1000 us
    reduce_scatter x1, waiting for transfers between devices, on_device(): lax.psum_scatter(jnp.einsum('td,tgf->dgf', columns, d_proj_low, preferred...  546 us
    all_gather x1, blocking collectives, on_device(): lax.all_gather(ffn_gain, 'fsdp', axis=0, tiled=True)  415 us
    reduce_scatter x1, waiting for transfers between devices, on_device(): lax.psum_scatter(contract_rows(hidden, d_out_low).astype(jnp.bfloat16), '...  260 us
    reduce_scatter x1, waiting for transfers between devices, on_device(): lax.psum_scatter(qkv_term.astype(jnp.bfloat16), 'fsdp', scatter_dimension...  122 us
    reduce_scatter x1, waiting for transfers between devices, on_device(): lax.psum_scatter(out_term.astype(jnp.bfloat16), 'fsdp', scatter_dimension...  91.1 us
    all_gather x1, waiting for transfers between devices, on_device(): lax.all_gather(qkv_weight, 'fsdp', axis=0, tiled=True)  77.8 us
    unnamed x118, local copies, waits for them, and re-layouts  74.5 us
  transfers between devices with their start and end apart: 14, of which 11 were waited for; matrix products, arithmetic and copies ran while one was open for 9% of the time, Pallas kernels for 0%

profile of v1, /device:TPU:0, one launch (start us, length us, event | category | flops | bytes accessed | tf_op | source)
XLA Modules:
  0.0 3138.1 jit_solution(1857989905166265707)
XLA Ops:
  8.6 22.5 all-gather
  34.2 77.8 %all-gather.8.cloned.1.call-done = bf16[2048,1536]{1,0:T(8,128)(2,1)} async-done(((bf16[256,1536]{1,0:T(8,128)(2,1)}), bf16[2048,1536]{1,0:T(8,128)(2,1)}) %all-gather.8.cloned.1.call-update) | async-done | bytes 6291472 | tf_op jit(solution)/shard_map/all_gather | solution.py:107
  131.3 107.2 %collective-permute-done = bf16[256,2,4096]{2,0,1:T(8,128)(2,1)} collective-permute-done((bf16[256,2,4096]{2,0,1:T(8,128)(2,1)}, bf16[256,2,4096]{2,0,1:T(8,128)(2,1)}, u32[]{:S(2)}, u32[]{:S(2)}) %collective-permute-start) | collective-permute-done | bytes 4194336 | tf_op jit(solution)/shard_map/ppermute | solution.py:18
  247.3 212.4 %collective-permute-done.1 = bf16[512,2,4096]{2,0,1:T(8,128)(2,1)S(1)} collective-permute-done((bf16[512,2,4096]{2,0,1:T(8,128)(2,1)}, bf16[512,2,4096]{2,0,1:T(8,128)(2,1)S(1)}, u32[]{:S(2)}, u32[]{:S(2)}) %collective-permute-start.1) | collective-permute-done | bytes 8388640 | tf_op jit(solution)/shard_map/ppermute | solution.py:18
  473.7 414.8 %all-gather.1 = bf16[8,1,256]{2,1,0:T(2,128)(2,1)S(1)} all-gather(bf16[1,1,256]{2,1,0:T(2,128)(2,1)S(1)} %reshape.283), channel_id=1, replica_groups=mesh['fsdp'=8,'ctx'=4] {'fsdp'}, dimensions={0}, use_global_device_ids=true | all-gather | bytes 4608 | tf_op jit(solution)/shard_map/all_gather | solution.py:110
  911.3 25.3 while.47
  956.7 680.8 %collective-permute-done.2 = bf16[1024,2,4096]{2,0,1:T(8,128)(2,1)} collective-permute-done((bf16[1024,2,4096]{2,0,1:T(8,128)(2,1)}, bf16[1024,2,4096]{2,0,1:T(8,128)(2,1)}, u32[]{:S(2)}, u32[]{:S(2)}) %collective-permute-start.2) | collective-permute-done | bytes 16777248 | tf_op jit(solution)/shard_map/ppermute | solution.py:18
  1637.5 14.6 constant_dynamic-update-slice_fusion.5
  1669.5 14.0 constant_dynamic-update-slice_fusion.1
  1683.5 18.2 fusion.72
  1715.0 71.4 %all-gather.16.cloned.1.call-done = bf16[2048,2,4096]{2,0,1:T(8,128)(2,1)} async-done(((bf16[256,2,4096]{2,0,1:T(8,128)(2,1)}), bf16[2048,2,4096]{2,0,1:T(8,128)(2,1)}) %all-gather.16.cloned.1.call-update) | async-done | bytes 33554448 | tf_op jit(solution)/shard_map/all_gather | solution.py:216
  1786.4 19.0 multiply_reduce_fusion
  1812.7 41.0 %while.46 = (s32[]{:T(128)}, bf16[2,512,512]{2,1,0:T(8,128)(2,1)}, s32[2]{0:T(128)S(1)}, s32[]{:T(128)}, bf16[2,512,2,4,64]{1,4,3,2,0:T(8,128)(2,1)S(1)}, /*inde...) while((s32[]{:T(128)}, bf16[2,512,512]{2,1,0:T(8,128)(2,1)}, ...), condition=%wide.region_13.14_spmd.clone, body=%wide.region_12.13_spmd.clone.sunk | while | flops 1096288000 | bytes 32956044 | solution.py:276
  1871.1 30.5 while.49
  1907.2 18.3 reduce-scatter.6.cloned.1.call-done
  1933.9 18.8 convolution_convert_fusion
  1952.8 259.7 %reduce-scatter.14.cloned.1.call-done = bf16[512,2048]{1,0:T(8,128)(2,1)} async-done(((bf16[4096,2048]{1,0:T(8,128)(2,1)}), bf16[512,2048]{1,0:T(8,128)(2,1)}) %reduce-scatter.14.cloned.1.call-update) | async-done | bytes 2097168 | tf_op jit(solution)/shard_map/reduce_scatter | solution.py:196
  2212.6 91.1 %reduce-scatter.10.cloned.1.call-done = bf16[128,2048]{1,0:T(8,128)(2,1)} async-done(((bf16[1024,2048]{1,0:T(8,128)(2,1)}), bf16[128,2048]{1,0:T(8,128)(2,1)}) %reduce-scatter.10.cloned.1.call-update) | async-done | bytes 524304 | tf_op jit(solution)/shard_map/reduce_scatter | solution.py:296
  2303.7 121.8 %reduce-scatter.8.cloned.1.call-done = bf16[256,1536]{1,0:T(8,128)(2,1)} async-done(((bf16[2048,1536]{1,0:T(8,128)(2,1)}), bf16[256,1536]{1,0:T(8,128)(2,1)}) %reduce-scatter.8.cloned.1.call-update) | async-done | bytes 786448 | tf_op jit(solution)/shard_map/reduce_scatter | solution.py:293
  2425.5 546.2 %reduce-scatter.12.cloned.1.call-done = bf16[256,2,4096]{2,0,1:T(8,128)(2,1)} async-done(((bf16[2048,2,4096]{2,0,1:T(8,128)(2,1)}), bf16[256,2,4096]{2,0,1:T(8,128)(2,1)}) %reduce-scatter.12.cloned.1.call-update) | async-done | bytes 4194320 | tf_op jit(solution)/shard_map/reduce_scatter | solution.py:205
  2973.0 15.3 fusion.85
  2995.2 19.0 all-reduce.13
  3022.7 37.9 %psum.55 = f32[2,64]{1,0:T(2,128)} all-reduce(f32[2,64]{1,0:T(2,128)S(1)} %pad_add_fusion.2), channel_id=1, replica_groups=mesh['fsdp'=8,'ctx'=4] {'fsdp','ctx'}, use_global_device_ids=true, to_apply=%region_36.37 | all-reduce | flops 128 | bytes 1024 | tf_op jit(solution)/shard_map/psum | solution.py:314
  3064.5 51.8 %all-reduce.18.cloned.1.call-done = (bf16[256,2,4096]{2,0,1:T(8,128)(2,1)}, bf16[256,1536]{1,0:T(8,128)(2,1)}, bf16[128,2048]{1,0:T(8,128)(2,1)}, bf16[512,2048]{1,0:T(8,128)(2,1)}) async-done(((bf16[256,2,4096]{2,0,1:T(8,128)(2,1)}, bf16[256,1536]{1,0:T(8,128)(2,1)}, bf16[128,2048]{1,0:T(8,128)(2,1)}, bf16[512,2048]{1,0:T(8,128)(2,1)}), (bf16[256,2,4096]{2,0,1:T(8,128)(2,1)}, bf16[256,1536]{1,0:T(8,128)(2,1)}, ...) | async-done | bytes 7602192 | tf_op jit(solution)/shard_map/psum | solution.py:309
  (296 shorter events, 302.3 us)
Async XLA Ops:
  7.2 104.8 %all-gather.8.cloned.1.call-start = ((), (), s32[]{:S(2)}) async-start(), calls=%async_computation.5 | async-start | bytes 7077888 | tf_op jit(solution)/shard_map/all_gather | solution.py:107
  7.9 895.8 %all-gather.10.cloned.1.call-start = ((), (), s32[]{:S(2)}) async-start(), calls=%async_computation.6 | async-start | bytes 1310720 | tf_op jit(solution)/shard_map/all_gather | solution.py:126
  31.1 85.8 %copy-start.30 = (f32[8,1,256]{2,1,0:T(1,128)}, f32[8,1,256]{2,1,0:T(1,128)S(1)}, u32[]{:S(2)}) copy-start(f32[8,1,256]{2,1,0:T(1,128)S(1)} %convert_element_type.220) | copy-start | bytes 24580
  34.0 860.8 %copy-start.46 = (f32[64]{0:T(128)}, f32[64]{0:T(128)S(1)}, u32[]{:S(2)}) copy-start(f32[64]{0:T(128)S(1)} %get-tuple-element.563) | copy-start | bytes 772
  34.2 861.5 %copy-start.22 = (f32[256,32]{0,1:T(8,128)}, f32[256,32]{0,1:T(8,128)S(1)}, u32[]{:S(2)}) copy-start(f32[256,32]{0,1:T(8,128)S(1)} %get-tuple-element.561) | copy-start | bytes 98308
  34.2 861.5 %copy-start.24 = (f32[256,32]{0,1:T(8,128)}, f32[256,32]{0,1:T(8,128)S(1)}, u32[]{:S(2)}) copy-start(f32[256,32]{0,1:T(8,128)S(1)} %get-tuple-element.562) | copy-start | bytes 98308
  119.8 831.8 %all-gather.12.cloned.1.call-start = ((), (), s32[]{:S(2)}) async-start(), calls=%async_computation.7 | async-start | bytes 4718592 | tf_op jit(solution)/shard_map/all_gather | solution.py:108
  120.6 1581.2 %all-gather.14.cloned.1.call-start = ((), (), s32[]{:S(2)}) async-start(), calls=%async_computation.8 | async-start | bytes 18874368 | tf_op jit(solution)/shard_map/all_gather | solution.py:190
  121.1 1665.3 %all-gather.16.cloned.1.call-start = ((), (), s32[]{:S(2)}) async-start(), calls=%async_computation.9 | async-start | bytes 37748736 | tf_op jit(solution)/shard_map/all_gather | solution.py:216
  129.7 1795.9 %reduce-scatter.6.cloned.1.call-start = ((), (), s32[]{:S(2)}) async-start(), calls=%async_computation.10 | async-start | bytes 1310720 | tf_op jit(solution)/shard_map/reduce_scatter | solution.py:275
  129.8 108.7 %collective-permute-start = (bf16[256,2,4096]{2,0,1:T(8,128)(2,1)}, bf16[256,2,4096]{2,0,1:T(8,128)(2,1)}, u32[]{:S(2)}, u32[]{:S(2)}) collective-permute-start(bf16[256,2,4096]{2,0,1:T(8,128)(2,1)} %get-tuple-element.549), channel_id=1, source_target_pairs={{0,28},{4,0},{8,4},{12,8},{16,12},{20,16},{24,20},{28,24},{1,29},{... | collective-permute-start | bytes 12582920 | tf_op jit(solution)/shard_map/ppermute | solution.py:18
  246.4 227.2 %copy-start.50 = (bf16[256]{0:T(256)(128)(2,1)S(1)}, bf16[256]{0:T(256)(128)(2,1)}, u32[]{:S(2)}) copy-start(bf16[256]{0:T(256)(128)(2,1)} %param.26) | copy-start | bytes 1540
  246.4 213.3 %collective-permute-start.1 = (bf16[512,2,4096]{2,0,1:T(8,128)(2,1)}, bf16[512,2,4096]{2,0,1:T(8,128)(2,1)S(1)}, u32[]{:S(2)}, u32[]{:S(2)}) collective-permute-start(bf16[512,2,4096]{2,0,1:T(8,128)(2,1)} %pad_maximum_fusion.1), channel_id=1, source_target_pairs={{0,24},{4,28},{8,0},{12,4},{16,8},{20,12},{24,16},{28,20},{1,25},{... | collective-permute-start | bytes 25165832 | tf_op jit(solution)/shard_map/ppermute | solution.py:18
  472.3 1165.2 %collective-permute-start.2 = (bf16[1024,2,4096]{2,0,1:T(8,128)(2,1)}, bf16[1024,2,4096]{2,0,1:T(8,128)(2,1)}, u32[]{:S(2)}, u32[]{:S(2)}) collective-permute-start(bf16[1024,2,4096]{2,0,1:T(8,128)(2,1)} %pad_maximum_fusion), channel_id=1, source_target_pairs={{0,16},{4,20},{8,24},{12,28},{16,0},{20,4},{24,8},{28,12},{1,17},{... | collective-permute-start | bytes 50331656 | tf_op jit(solution)/shard_map/ppermute | solution.py:18
  889.2 964.6 %copy-start.48 = (f32[256]{0:T(256)}, f32[256]{0:T(256)S(1)}, u32[]{:S(2)}) copy-start(f32[256]{0:T(256)S(1)} %compare_convert_fusion) | copy-start | bytes 3076
  956.7 848.7 %copy-start.38 = (f32[256]{0:T(256)}, f32[256]{0:T(256)S(1)}, u32[]{:S(2)}) copy-start(f32[256]{0:T(256)S(1)} %fusion.117) | copy-start | bytes 3076
  956.7 695.4 %copy-start.9 = (bf16[256,2,4096]{2,1,0:T(2,128)(2,1)S(1)}, bf16[256,2,4096]{2,1,0:T(2,128)(2,1)}, u32[]{:S(2)}) copy-start(bf16[256,2,4096]{2,1,0:T(2,128)(2,1)} %param.23) | copy-start | bytes 12582916
  1853.8 358.8 %reduce-scatter.14.cloned.1.call-start = ((), (), s32[]{:S(2)}) async-start(), calls=%async_computation.14 | async-start | bytes 18874368 | tf_op jit(solution)/shard_map/reduce_scatter | solution.py:196
  1865.1 438.6 %reduce-scatter.10.cloned.1.call-start = ((), (), s32[]{:S(2)}) async-start(), calls=%async_computation.12 | async-start | bytes 4718592 | tf_op jit(solution)/shard_map/reduce_scatter | solution.py:296
  1871.0 554.5 %reduce-scatter.8.cloned.1.call-start = ((), (), s32[]{:S(2)}) async-start(), calls=%async_computation.11 | async-start | bytes 7077888 | tf_op jit(solution)/shard_map/reduce_scatter | solution.py:293
  1932.4 1039.3 %reduce-scatter.12.cloned.1.call-start = ((), (), s32[]{:S(2)}) async-start(), calls=%async_computation.13 | async-start | bytes 37748736 | tf_op jit(solution)/shard_map/reduce_scatter | solution.py:205
  1952.8 1019.0 %copy-start.51 = (u32[32]{0:T(128)S(1)}, u32[32]{0:T(128)}, u32[]{:S(2)}) copy-start(u32[32]{0:T(128)} %constant.151) | copy-start | bytes 388
  1952.8 1020.2 %copy-start.49 = (f32[256]{0:T(256)S(1)}, f32[256]{0:T(256)}, u32[]{:S(2)}) copy-start(f32[256]{0:T(256)} %copy-done.48) | copy-start | bytes 3076
  1952.8 1163.5 %all-reduce.18.cloned.1.call-start = ((), (), s32[]{:S(2)}) async-start(), calls=%async_computation.15 | async-start | bytes 15204352 | tf_op jit(solution)/shard_map/psum | solution.py:309
  (42 other events, 716.6 us)
Sparse Core Ops, SparseCore 0:
  10.2 101.7 all-gather.7
  119.9 14.8 all-gather.9
  137.0 171.7 all-gather.11
  310.8 836.8 all-gather.13
  1149.7 636.6 all-gather.15
  1853.9 71.6 reduce-scatter.5
  1929.8 282.7 reduce-scatter.13
  2216.8 86.8 reduce-scatter.9
  2307.7 117.7 reduce-scatter.7
  2429.6 542.0 reduce-scatter.11
  2974.4 141.8 all-reduce.17
